TPU v7x, 256 devices: a whole 4x4x8 slice. The times are simulated.
256 devices in a mesh: tile: 8 (over y, core), plane: 32 (over x, z).
Axes of the slice: x: 4, y: 4, z: 8, core: 2. Of those that a mesh axis runs over, the one named last changes fastest.
Arguments:
- observed: float32 [2, 32, 512, 256], P(None, 'plane', 'tile'), may hold values from 0.5 to 4
- intersection_strip: float32 [2, 32, 256, 256], P(None, 'plane', 'tile'), may hold values from 0.5 to 4
- axial_taps: float32 [2, 41], replicated, may hold values from 0.05 to 1
- lateral_taps: float32 [2, 15], replicated, may hold values from 0.05 to 1
- extents: int32 [8], P('tile'), may hold values from 1 to 32, as said below
- section_skews: int32 [8], P('tile'), may hold values from 0 to 255
Outputs:
- estimate: float32 [2, 32, 512, 256], P(None, 'plane', 'tile')
Inputs may be any that keep to these rules, and one draw needn't show every extreme that they name: `extents`: entry 0 is not used; the largest of the entries 1 to 7 is 32.
All inputs are finite; a program needn't handle non-finite values.
Results may differ from a plain program's by a relative error of at most 0.00005.
Values sent between devices are 32-bit elements; how exact they have to be, the bound alone decides.
A program may use at most 64 MiB of HBM per device.

v0:
```python
import jax
import jax.numpy as jnp
from jax import lax
from jax.sharding import PartitionSpec as P

ITERS = 2
highest = lax.Precision.HIGHEST


def with_halo(block, sides, width):
    for axis, dim in sides:
        count = lax.axis_size(axis)
        forward = [(i, i + 1) for i in range(count - 1)]
        backward = [(target, source) for source, target in forward]
        low = lax.ppermute(
            lax.slice_in_dim(block, block.shape[dim] - width, None, axis=dim), axis, forward
        )
        high = lax.ppermute(lax.slice_in_dim(block, 0, width, axis=dim), axis, backward)
        block = jnp.concatenate([low, block, high], axis=dim)
    return block


def from_behind(array, axis, by):
    length = lax.axis_size(axis)
    pairs = [(i, i + by) for i in range(length) if 0 <= i + by < length]
    return lax.ppermute(array, axis, pairs)


def band_matrix(kernel, row_count, col_count, offset):
    offsets = (
        jnp.arange(col_count, dtype=jnp.int32)[None, :]
        - jnp.arange(row_count, dtype=jnp.int32)[:, None]
        + offset
    )
    tap_ids = jnp.arange(kernel.shape[1], dtype=jnp.int32)
    one_hot = jnp.where(offsets[:, :, None] == tap_ids[None, None, :], 1.0, 0.0).astype(jnp.float32)
    return jnp.einsum("ck,rsk->crs", kernel, one_hot, precision=highest)


def blur_rows_x(volume, x_band):
    chans, planes, rowsn, voxels = volume.shape
    blocks = volume.reshape(chans, planes, rowsn, voxels // 128, 128)
    padded = jnp.pad(blocks, ((0, 0), (0, 0), (0, 0), (1, 1), (0, 0)))
    window = jnp.concatenate(
        [padded[:, :, :, :-2], padded[:, :, :, 1:-1], padded[:, :, :, 2:]], axis=4
    )
    result = jnp.einsum("czynw,cow->czyno", window, x_band, precision=highest)
    return result.reshape(chans, planes, rowsn, voxels)


def blur_rows_y(volume, y_band, half_width):
    padded = with_halo(volume, (("tile", 2),), half_width)
    return jnp.einsum("cyp,czpx->czyx", y_band, padded, precision=highest)


def axial_pass(pencils, z_band):
    return jnp.einsum("cij,cjw->ciw", z_band, pencils, precision=highest)


def to_pencils(volume):
    chans, planes, rowsn, voxels = volume.shape
    return lax.all_to_all(
        volume.reshape(chans, planes, rowsn * voxels),
        "plane",
        split_axis=2,
        concat_axis=1,
        tiled=True,
    )


def to_planes(pencils, row_count, col_count):
    flattened = lax.all_to_all(pencils, "plane", split_axis=1, concat_axis=2, tiled=True)
    return flattened.reshape(flattened.shape[0], flattened.shape[1], row_count, col_count)


def shards(observed, intersection_strip, axial_taps, lateral_taps, extents, section_skews):
    chans, planes, row_count, col_count = observed.shape
    strip_count = intersection_strip.shape[2]
    received = from_behind(intersection_strip, "tile", 1)
    turned = jnp.roll(received, section_skews[0], axis=3)
    reach_rows = jnp.where(lax.axis_index("tile") == 0, 0, extents[0])
    inside = (jnp.arange(strip_count, dtype=jnp.int32) < reach_rows)[None, None, :, None]
    top_rows = observed[:, :, :strip_count]
    joined_obs = jnp.concatenate(
        [jnp.where(inside, 0.5 * (top_rows + turned), top_rows), observed[:, :, strip_count:]],
        axis=2,
    )
    axial_width = axial_taps.shape[1]
    lateral_width = lateral_taps.shape[1]
    axial_half = axial_width // 2
    lateral_half = lateral_width // 2
    total_planes = planes * lax.axis_size("plane")
    axial_flip = jnp.flip(axial_taps, axis=1)
    lateral_flip = jnp.flip(lateral_taps, axis=1)
    z_forward = band_matrix(axial_taps, total_planes, total_planes, axial_half)
    z_adjoint = band_matrix(axial_flip, total_planes, total_planes, axial_half)
    y_forward = band_matrix(lateral_taps, row_count, row_count + 2 * lateral_half, 0)
    y_adjoint = band_matrix(lateral_flip, row_count, row_count + 2 * lateral_half, 0)
    x_forward = band_matrix(lateral_taps, 128, 384, lateral_half - 128)
    x_adjoint = band_matrix(lateral_flip, 128, 384, lateral_half - 128)
    estimate = joined_obs
    for sweep in range(ITERS):
        lateral_done = blur_rows_y(blur_rows_x(estimate, x_forward), y_forward, lateral_half)
        blurred = to_planes(axial_pass(to_pencils(lateral_done), z_forward), row_count, col_count)
        quotient = joined_obs / blurred
        spread_back = to_planes(axial_pass(to_pencils(quotient), z_adjoint), row_count, col_count)
        estimate = estimate * blur_rows_x(
            blur_rows_y(spread_back, y_adjoint, lateral_half), x_adjoint
        )
    return estimate


def solution(mesh):
    in_specs = (
        P(None, "plane", "tile", None),
        P(None, "plane", "tile", None),
        P(),
        P(),
        P("tile"),
        P("tile"),
    )
    out_specs = P(None, "plane", "tile", None)
    return jax.shard_map(shards, mesh=mesh, in_specs=in_specs, out_specs=out_specs, check_vma=False)
```

profile of v0, /device:TPU:1, one launch (start us, length us, event | category | flops | bytes accessed | tf_op | source)
XLA Modules:
  0.0 619.2 jit_solution(13503194051513561913)
XLA Ops:
  0.0 4.6 collective-permute-start
  6.0 3.3 fusion.10
  11.3 1.9 collective-permute-start.1
  13.3 2.4 collective-permute-start.2
  16.9 1.4 collective-permute-done.2
  18.6 4.6 copy.141
  23.8 74.4 %reduce = f32[16384,2]{1,0:T(8,128)} reduce(f32[16384,1,2]{2,1,0:T(1,128)} %bitcast.131, f32[]{:T(128)} %broadcast.47), dimensions={1}, to_apply=%bitcast.113.reduce_sub_computation | reduce | bytes 262148
  98.2 8.2 %reshape.294 = f32[32,1,1024]{2,1,0:T(1,128)} reshape(f32[16384,2]{1,0:T(8,128)} %reduce) | data formatting | bytes 262144
  106.4 11.2 %all-to-all-start = ((f32[32,1,1024]{2,1,0:T(1,128)}), f32[32,1,1024]{2,1,0:T(1,128)S(1)}, u32[]{:S(2)}, u32[]{:S(2)}) async-start(f32[32,1,1024]{2,1,0:T(1,128)} %reshape.294), calls=%async_computation | async-start | bytes 262144 | tf_op jit(solution)/shard_map/all_to_all | solution.py:62
  117.7 2.2 convolution_bitcast_fusion.6
  119.9 7.5 %all-to-all-done = f32[32,1,1024]{2,1,0:T(1,128)S(1)} async-done(((f32[32,1,1024]{2,1,0:T(1,128)}), f32[32,1,1024]{2,1,0:T(1,128)S(1)}, u32[]{:S(2)}, u32[]{:S(2)}) %all-to-all-start) | async-done | bytes 131104 | tf_op jit(solution)/shard_map/all_to_all | solution.py:62
  128.3 14.9 %reshape.295 = f32[16384,1,2]{2,1,0:T(1,128)} reshape(f32[32,1024]{1,0:T(8,128)S(1)} %reduce.1) | data formatting | bytes 262144
  143.2 5.2 copy.142
  149.5 3.9 all-to-all-start.1
  153.5 9.1 %all-to-all-done.1 = f32[2,32,512]{2,0,1:T(2,128)S(1)} async-done(((f32[2,32,512]{2,0,1:T(2,128)}), f32[2,32,512]{2,0,1:T(2,128)S(1)}, u32[]{:S(2)}, u32[]{:S(2)}) %all-to-all-start.1) | async-done | bytes 131104 | tf_op jit(solution)/shard_map/all_to_all | solution.py:72
  162.6 12.1 %copy.105 = f32[2,1,16384]{0,1,2:T(1,128)} copy(f32[2,1,16384]{2,0,1:T(2,128)S(1)} %div.24) | data formatting | bytes 262144 | tf_op jit(solution)/shard_map/div | solution.py:105
  174.7 74.4 %reduce.2 = f32[16384,2]{1,0:T(8,128)} reduce(f32[16384,1,2]{2,1,0:T(1,128)} %bitcast.132, f32[]{:T(128)} %broadcast.47), dimensions={1}, to_apply=%bitcast.115.reduce_sub_computation | reduce | bytes 262148
  249.1 8.2 %reshape.296 = f32[32,1,1024]{2,1,0:T(1,128)} reshape(f32[16384,2]{1,0:T(8,128)} %reduce.2) | data formatting | bytes 262144
  257.4 4.8 all-to-all-start.2
  262.2 2.2 convolution_bitcast_fusion.7
  264.4 6.9 %all-to-all-done.2 = f32[32,1,1024]{2,1,0:T(1,128)S(1)} async-done(((f32[32,1,1024]{2,1,0:T(1,128)}), f32[32,1,1024]{2,1,0:T(1,128)S(1)}, u32[]{:S(2)}, u32[]{:S(2)}) %all-to-all-start.2) | async-done | bytes 131104 | tf_op jit(solution)/shard_map/all_to_all | solution.py:62
  272.2 14.9 %reshape.297 = f32[16384,1,2]{2,1,0:T(1,128)} reshape(f32[32,1024]{1,0:T(8,128)S(1)} %reduce.3) | data formatting | bytes 262144
  287.1 5.2 copy.143
  293.4 3.9 all-to-all-start.3
  297.8 8.5 %all-to-all-done.3 = f32[2,32,512]{2,0,1:T(2,128)S(1)} async-done(((f32[2,32,512]{2,0,1:T(2,128)}), f32[2,32,512]{2,0,1:T(2,128)S(1)}, u32[]{:S(2)}, u32[]{:S(2)}) %all-to-all-start.3) | async-done | bytes 131104 | tf_op jit(solution)/shard_map/all_to_all | solution.py:72
  306.4 7.1 %collective-permute-start.3 = (f32[2,1,7,256]{3,2,0,1:T(8,128)S(1)}, f32[2,1,7,256]{3,2,0,1:T(8,128)S(1)}, u32[]{:S(2)}, u32[]{:S(2)}) collective-permute-start(f32[2,1,7,256]{3,2,0,1:T(8,128)S(1)} %get-tuple-element.15), channel_id=1, source_target_pairs={{0,32},{32,64},{64,96},{96,128},{128,160},{160,192},{192,224},{1,3... | collective-permute-start | bytes 43016 | tf_op jit(solution)/shard_map/ppermute | solution.py:15
  313.6 1.9 collective-permute-start.4
  315.5 2.6 fusion.13
  320.6 3.3 collective-permute-start.5
  323.9 2.3 collective-permute-start.6
  326.2 2.7 collective-permute-done.6
  329.2 4.6 copy.148
  333.8 74.4 %reduce.4 = f32[16384,2]{1,0:T(8,128)} reduce(f32[16384,1,2]{2,1,0:T(1,128)} %bitcast.133, f32[]{:T(128)} %broadcast.47), dimensions={1}, to_apply=%bitcast.117.reduce_sub_computation | reduce | bytes 262148
  408.3 7.6 %reshape.298 = f32[32,1,1024]{2,1,0:T(1,128)S(1)} reshape(f32[16384,2]{1,0:T(8,128)} %reduce.4) | data formatting | bytes 262144
  415.9 12.5 %all_to_all.84 = f32[32,1,1024]{2,1,0:T(1,128)S(1)} all-to-all(f32[32,1,1024]{2,1,0:T(1,128)S(1)} %reshape.298), channel_id=1, replica_groups=mesh['tile'=8,'plane'=32] {'plane'}, dimensions={0} | all-to-all | bytes 262144 | tf_op jit(solution)/shard_map/all_to_all | solution.py:62
  429.3 14.9 %reshape.299 = f32[16384,1,2]{2,1,0:T(1,128)} reshape(f32[32,1024]{1,0:T(8,128)S(1)} %reduce.5) | data formatting | bytes 262144
  444.2 5.2 copy.149
  449.8 12.7 %all_to_all.85 = f32[2,32,512]{2,0,1:T(2,128)S(1)} all-to-all(f32[2,32,512]{2,0,1:T(2,128)S(1)} %copy.123), channel_id=1, replica_groups=mesh['tile'=8,'plane'=32] {'plane'}, dimensions={1} | all-to-all | bytes 262144 | tf_op jit(solution)/shard_map/all_to_all | solution.py:72
  462.5 12.1 %copy.124 = f32[2,1,16384]{0,1,2:T(1,128)} copy(f32[2,1,16384]{2,0,1:T(2,128)S(1)} %div.25) | data formatting | bytes 262144 | tf_op jit(solution)/shard_map/div | solution.py:105
  474.6 74.4 %reduce.6 = f32[16384,2]{1,0:T(8,128)} reduce(f32[16384,1,2]{2,1,0:T(1,128)} %bitcast.134, f32[]{:T(128)} %broadcast.47), dimensions={1}, to_apply=%bitcast.119.reduce_sub_computation | reduce | bytes 262148
  549.1 7.6 %reshape.300 = f32[32,1,1024]{2,1,0:T(1,128)S(1)} reshape(f32[16384,2]{1,0:T(8,128)} %reduce.6) | data formatting | bytes 262144
  556.7 13.6 %all_to_all.86 = f32[32,1,1024]{2,1,0:T(1,128)S(1)} all-to-all(f32[32,1,1024]{2,1,0:T(1,128)S(1)} %reshape.300), channel_id=1, replica_groups=mesh['tile'=8,'plane'=32] {'plane'}, dimensions={0} | all-to-all | bytes 262144 | tf_op jit(solution)/shard_map/all_to_all | solution.py:62
  571.2 14.9 %reshape.301 = f32[16384,1,2]{2,1,0:T(1,128)} reshape(f32[32,1024]{1,0:T(8,128)S(1)} %reduce.7) | data formatting | bytes 262144
  586.1 5.2 copy.150
  591.7 12.7 %all_to_all.87 = f32[2,32,512]{2,0,1:T(2,128)S(1)} all-to-all(f32[2,32,512]{2,0,1:T(2,128)S(1)} %copy.127), channel_id=1, replica_groups=mesh['tile'=8,'plane'=32] {'plane'}, dimensions={1} | all-to-all | bytes 262144 | tf_op jit(solution)/shard_map/all_to_all | solution.py:72
  604.5 7.6 %collective-permute-start.7 = (f32[2,1,7,256]{3,2,0,1:T(8,128)S(1)}, f32[2,1,7,256]{3,2,0,1:T(8,128)S(1)}, u32[]{:S(2)}, u32[]{:S(2)}) collective-permute-start(f32[2,1,7,256]{3,2,0,1:T(8,128)S(1)} %get-tuple-element.7), channel_id=1, source_target_pairs={{0,32},{32,64},{64,96},{96,128},{128,160},{160,192},{192,224},{1,3... | collective-permute-start | bytes 43016 | tf_op jit(solution)/shard_map/ppermute | solution.py:15
  612.1 1.9 collective-permute-start.8
  614.2 2.9 collective-permute-done.8
  (74 shorter events, 16.2 us)
Async XLA Ops:
  0.0 9.3 %collective-permute-start = (f32[2,1,32,256]{3,2,0,1:T(8,128)}, f32[2,1,32,256]{3,2,0,1:T(8,128)S(1)}, u32[]{:S(2)}, u32[]{:S(2)}) collective-permute-start(f32[2,1,32,256]{3,2,0,1:T(8,128)} %bitcast.146), channel_id=1, source_target_pairs={{0,32},{32,64},{64,96},{96,128},{128,160},{160,192},{192,224},{1,3... | collective-permute-start | bytes 196616 | tf_op jit(solution)/shard_map/ppermute | solution.py:26
  11.3 5.5 collective-permute-start.1
  13.3 5.1 collective-permute-start.2
  98.2 19.5 %copy-start = (f32[2,41]{1,0:T(2,128)S(1)}, f32[2,41]{1,0:T(2,128)}, u32[]{:S(2)}) copy-start(f32[2,41]{1,0:T(2,128)} %param.8) | copy-start | bytes 988
  106.4 21.0 %all-to-all-start = ((f32[32,1,1024]{2,1,0:T(1,128)}), f32[32,1,1024]{2,1,0:T(1,128)S(1)}, u32[]{:S(2)}, u32[]{:S(2)}) async-start(f32[32,1,1024]{2,1,0:T(1,128)} %reshape.294), calls=%async_computation | async-start | bytes 262144 | tf_op jit(solution)/shard_map/all_to_all | solution.py:62
  149.5 13.0 %all-to-all-start.1 = ((f32[2,32,512]{2,0,1:T(2,128)}), f32[2,32,512]{2,0,1:T(2,128)S(1)}, u32[]{:S(2)}, u32[]{:S(2)}) async-start(f32[2,32,512]{2,0,1:T(2,128)} %copy.104), calls=%async_computation.1 | async-start | bytes 262144 | tf_op jit(solution)/shard_map/all_to_all | solution.py:72
  257.4 13.9 %all-to-all-start.2 = ((f32[32,1,1024]{2,1,0:T(1,128)}), f32[32,1,1024]{2,1,0:T(1,128)S(1)}, u32[]{:S(2)}, u32[]{:S(2)}) async-start(f32[32,1,1024]{2,1,0:T(1,128)} %reshape.296), calls=%async_computation.2 | async-start | bytes 262144 | tf_op jit(solution)/shard_map/all_to_all | solution.py:62
  272.2 25.0 %copy-start.1 = (f32[2,15]{1,0:T(2,128)S(1)}, f32[2,15]{1,0:T(2,128)}, u32[]{:S(2)}) copy-start(f32[2,15]{1,0:T(2,128)} %param.9) | copy-start | bytes 364
  293.4 13.0 %all-to-all-start.3 = ((f32[2,32,512]{2,0,1:T(2,128)}), f32[2,32,512]{2,0,1:T(2,128)S(1)}, u32[]{:S(2)}, u32[]{:S(2)}) async-start(f32[2,32,512]{2,0,1:T(2,128)} %copy.108), calls=%async_computation.3 | async-start | bytes 262144 | tf_op jit(solution)/shard_map/all_to_all | solution.py:72
  306.4 11.8 %collective-permute-start.3 = (f32[2,1,7,256]{3,2,0,1:T(8,128)S(1)}, f32[2,1,7,256]{3,2,0,1:T(8,128)S(1)}, u32[]{:S(2)}, u32[]{:S(2)}) collective-permute-start(f32[2,1,7,256]{3,2,0,1:T(8,128)S(1)} %get-tuple-element.15), channel_id=1, source_target_pairs={{0,32},{32,64},{64,96},{96,128},{128,160},{160,192},{192,224},{1,3... | collective-permute-start | bytes 43016 | tf_op jit(solution)/shard_map/ppermute | solution.py:15
  313.6 5.1 collective-permute-start.4
  320.6 5.6 collective-permute-start.5
  323.9 5.1 collective-permute-start.6
  604.5 9.8 %collective-permute-start.7 = (f32[2,1,7,256]{3,2,0,1:T(8,128)S(1)}, f32[2,1,7,256]{3,2,0,1:T(8,128)S(1)}, u32[]{:S(2)}, u32[]{:S(2)}) collective-permute-start(f32[2,1,7,256]{3,2,0,1:T(8,128)S(1)} %get-tuple-element.7), channel_id=1, source_target_pairs={{0,32},{32,64},{64,96},{96,128},{128,160},{160,192},{192,224},{1,3... | collective-permute-start | bytes 43016 | tf_op jit(solution)/shard_map/ppermute | solution.py:15
  612.1 5.1 collective-permute-start.8
where the time goes:
time: 628 us; the launch traced here: 619 us
  other arithmetic  303 us (48%)
  local copies, waits for them, and re-layouts  149 us (24%)
  starting transfers between devices  56.8 us (9%)
  blocking collectives  51.5 us (8%)
  waiting for transfers between devices  39.4 us (6%)
  matrix products  16.8 us (3%)
    unnamed x4, other arithmetic  298 us
    unnamed x13, local copies, waits for them, and re-layouts  91.8 us
    all_to_all x2, blocking collectives, to_pencils(): lax.all_to_all(volume.reshape(chans, planes, rowsn * voxels), 'plane', sp...  26.1 us
    all_to_all x2, blocking collectives, to_planes(): lax.all_to_all(pencils, 'plane', split_axis=1, concat_axis=2, tiled=True)  25.4 us
    div x2, local copies, waits for them, and re-layouts, shards(): quotient = joined_obs / blurred  24.2 us
    all_to_all x4, local copies, waits for them, and re-layouts, to_pencils(): lax.all_to_all(volume.reshape(chans, planes, rowsn * voxels), 'plane', sp...  20.8 us
    ppermute x4, starting transfers between devices, with_halo(): lax.ppermute(lax.slice_in_dim(block, block.shape[dim] - width, None, axis...  19.9 us
    all_to_all x2, waiting for transfers between devices, to_planes(): lax.all_to_all(pencils, 'plane', split_axis=1, concat_axis=2, tiled=True)  17.6 us
  transfers between devices with their start and end apart: 13, of which 8 were waited for; matrix products, arithmetic and copies ran while one was open for 2% of the time, Pallas kernels for 0%

commit v1 on v0

--- a/solution.py
+++ b/solution.py
@@ -59,12 +59,18 @@
 
 def to_pencils(volume):
     chans, planes, rowsn, voxels = volume.shape
-    return lax.all_to_all(
-        volume.reshape(chans, planes, rowsn * voxels),
-        "plane",
-        split_axis=2,
-        concat_axis=1,
-        tiled=True,
+    return jnp.concatenate(
+        lax.all_to_all(
+            jnp.stack(
+                jnp.split(
+                    volume.reshape(chans, planes, rowsn * voxels), lax.axis_size("plane"), axis=2
+                )
+            ),
+            "plane",
+            0,
+            0,
+        ),
+        axis=1,
     )
 
 

time: 628 us -> 210 us (0.33); the launches traced: 619 us -> 209 us
  other arithmetic: 303 us -> 1.03 us
  local copies, waits for them, and re-layouts: 149 us -> 41.9 us
    unnamed x4 -> x0, other arithmetic: 298 us -> none
    unnamed x13 -> x130, local copies, waits for them, and re-layouts: 91.8 us -> 37.3 us
    div x2 -> x0, local copies, waits for them, and re-layouts: 24.2 us -> none  [shards(): quotient = joined_obs / blurred]
    all_to_all x4 -> x0, local copies, waits for them, and re-layouts: 20.8 us -> none  [to_pencils(): lax.all_to_all(volume.reshape(chans, planes, rowsn * voxels), 'plane', sp...]
    reshape x2, local copies, waits for them, and re-layouts: 9.22 us -> 0.17 us  [to_pencils(): volume.reshape(chans, planes, rowsn * voxels)]
  transfers between devices with their start and end apart: 13 -> 13, of which waited for: 8 -> 8; matrix products, arithmetic and copies ran while one was open for 2% -> 6% of each run, Pallas kernels for 0% -> 0%
where the time goes in v1:
time: 210 us; the launch traced here: 209 us
  starting transfers between devices  56.4 us (27%)
  blocking collectives  51.3 us (24%)
  local copies, waits for them, and re-layouts  41.9 us (20%)
  waiting for transfers between devices  40.4 us (19%)
  matrix products  16.1 us (8%)
  between operations  2.18 us (1%)
    unnamed x130, local copies, waits for them, and re-layouts  37.3 us
    all_to_all x2, blocking collectives, to_pencils(): lax.all_to_all(jnp.stack(jnp.split(volume.reshape(chans, planes, rowsn *...  26.1 us
    all_to_all x2, blocking collectives, to_planes(): lax.all_to_all(pencils, 'plane', split_axis=1, concat_axis=2, tiled=True)  25.3 us
    ppermute x4, starting transfers between devices, with_halo(): lax.ppermute(lax.slice_in_dim(block, block.shape[dim] - width, None, axis...  20.1 us
    all_to_all x2, waiting for transfers between devices, to_planes(): lax.all_to_all(pencils, 'plane', split_axis=1, concat_axis=2, tiled=True)  17.6 us
    all_to_all x2, starting transfers between devices, to_pencils(): lax.all_to_all(jnp.stack(jnp.split(volume.reshape(chans, planes, rowsn *...  15.6 us
    all_to_all x2, waiting for transfers between devices, to_pencils(): lax.all_to_all(jnp.stack(jnp.split(volume.reshape(chans, planes, rowsn *...  14.4 us
    dot_general x6, matrix products, band_matrix(): return jnp.einsum('ck,rsk->crs', kernel, one_hot, precision=highest)  11.4 us
  transfers between devices with their start and end apart: 13, of which 8 were waited for; matrix products, arithmetic and copies ran while one was open for 6% of the time, Pallas kernels for 0%

profile of v1, /device:TPU:1, one launch (start us, length us, event | category | flops | bytes accessed | tf_op | source)
XLA Modules:
  0.0 209.3 jit_solution(3307490047827642545)
XLA Ops:
  0.0 4.6 %collective-permute-start = (f32[2,1,32,256]{3,2,0,1:T(8,128)}, f32[2,1,32,256]{3,2,0,1:T(8,128)S(1)}, u32[]{:S(2)}, u32[]{:S(2)}) collective-permute-start(f32[2,1,32,256]{3,2,0,1:T(8,128)} %bitcast.660), channel_id=1, source_target_pairs={{0,32},{32,64},{64,96},{96,128},{128,160},{160,192},{192,224},{1,3... | collective-permute-start | bytes 196616 | tf_op jit(solution)/shard_map/ppermute | solution.py:26
  6.0 3.4 %fusion.10 = f32[2,128,384,1]{2,0,1,3:T(2,128)S(1)} fusion(s32[128,384]{1,0:T(8,128)S(1)} %subtract_add_fusion, f32[2,15]{1,0:T(2,128)} %param.9), kind=kOutput, calls=%fused_computation.11 | convolution fusion | flops 19169280 | bytes 589944 | tf_op jit(solution)/shard_map/ck,rsk->crs/dot_general | solution.py:37
  9.6 0.6 fusion.20
  10.5 1.9 collective-permute-start.1
  12.5 2.4 %collective-permute-start.2 = (f32[2,1,7,256]{3,2,0,1:T(8,128)S(1)}, f32[2,1,7,256]{3,2,0,1:T(8,128)S(1)}, u32[]{:S(2)}, u32[]{:S(2)}) collective-permute-start(f32[2,1,7,256]{3,2,0,1:T(8,128)S(1)} %get-tuple-element.18), channel_id=1, source_target_pairs={{32,0},{64,32},{96,64},{128,96},{160,128},{192,160},{224,192},{33,... | collective-permute-start | bytes 43016 | tf_op jit(solution)/shard_map/ppermute | solution.py:18
  15.4 2.1 %collective-permute-done.2 = f32[2,1,7,256]{3,2,0,1:T(8,128)S(1)} collective-permute-done((f32[2,1,7,256]{3,2,0,1:T(8,128)S(1)}, f32[2,1,7,256]{3,2,0,1:T(8,128)S(1)}, u32[]{:S(2)}, u32[]{:S(2)}) %collective-permute-start.2) | collective-permute-done | bytes 14368 | tf_op jit(solution)/shard_map/ppermute | solution.py:18
  17.9 0.6 constant_dynamic-update-slice_fusion.31
  18.5 0.6 constant_dynamic-update-slice_fusion.30
  19.7 0.6 constant_dynamic-update-slice_fusion.28
  20.3 0.6 constant_dynamic-update-slice_fusion.27
  20.9 0.6 constant_dynamic-update-slice_fusion.26
  21.5 0.6 constant_dynamic-update-slice_fusion.25
  22.1 0.6 constant_dynamic-update-slice_fusion.24
  22.7 0.6 constant_dynamic-update-slice_fusion.23
  23.3 0.6 constant_dynamic-update-slice_fusion.22
  23.9 0.6 constant_dynamic-update-slice_fusion.21
  24.5 0.6 constant_dynamic-update-slice_fusion.20
  25.0 0.6 constant_dynamic-update-slice_fusion.19
  36.9 11.0 %all-to-all-start = ((f32[32,2,1,512]{3,1,2,0:T(2,128)}), f32[32,2,1,512]{3,1,2,0:T(2,128)S(1)}, u32[]{:S(2)}, u32[]{:S(2)}) async-start(f32[32,2,1,512]{3,1,2,0:T(2,128)} %constant_dynamic-update-slice_fusion), calls=%async_computation | async-start | bytes 262144 | tf_op jit(solution)/shard_map/all_to_all | solution.py:63
  48.0 2.2 %convolution_bitcast_fusion.6 = f32[2,32,32]{2,0,1:T(2,128)S(1)} fusion(s32[32,32]{1,0:T(8,128)S(1)} %subtract_add_fusion.1, f32[2,41]{1,0:T(2,128)S(1)} %copy-done.1), kind=kOutput, calls=%fused_computation.19 | convolution fusion | flops 1091584 | bytes 12616 | tf_op jit(solution)/shard_map/ck,rsk->crs/dot_general | solution.py:37
  50.2 7.6 %all-to-all-done = f32[32,2,1,512]{3,1,2,0:T(2,128)S(1)} async-done(((f32[32,2,1,512]{3,1,2,0:T(2,128)}), f32[32,2,1,512]{3,1,2,0:T(2,128)S(1)}, u32[]{:S(2)}, u32[]{:S(2)}) %all-to-all-start) | async-done | bytes 131104 | tf_op jit(solution)/shard_map/all_to_all | solution.py:63
  58.0 0.8 copy.326
  58.8 3.9 %all-to-all-start.1 = ((f32[2,32,512]{2,0,1:T(2,128)}), f32[2,32,512]{2,0,1:T(2,128)S(1)}, u32[]{:S(2)}, u32[]{:S(2)}) async-start(f32[2,32,512]{2,0,1:T(2,128)} %copy.326), calls=%async_computation.1 | async-start | bytes 262144 | tf_op jit(solution)/shard_map/all_to_all | solution.py:78
  62.7 9.0 %all-to-all-done.1 = f32[2,32,512]{2,0,1:T(2,128)S(1)} async-done(((f32[2,32,512]{2,0,1:T(2,128)}), f32[2,32,512]{2,0,1:T(2,128)S(1)}, u32[]{:S(2)}, u32[]{:S(2)}) %all-to-all-start.1) | async-done | bytes 131104 | tf_op jit(solution)/shard_map/all_to_all | solution.py:78
  71.9 0.6 constant_dynamic-update-slice_fusion.63
  90.9 4.5 %all-to-all-start.2 = ((f32[32,2,1,512]{3,1,2,0:T(2,128)}), f32[32,2,1,512]{3,1,2,0:T(2,128)S(1)}, u32[]{:S(2)}, u32[]{:S(2)}) async-start(f32[32,2,1,512]{3,1,2,0:T(2,128)} %constant_dynamic-update-slice_fusion.32), calls=%async_computation.2 | async-start | bytes 262144 | tf_op jit(solution)/shard_map/all_to_all | solution.py:63
  95.5 2.2 %convolution_bitcast_fusion.7 = f32[2,32,32]{2,0,1:T(2,128)S(1)} fusion(s32[32,32]{1,0:T(8,128)S(1)} %subtract_add_fusion.1, f32[2,41]{1,0:T(2,128)S(1)} %rev.8), kind=kOutput, calls=%fused_computation.20 | convolution fusion | flops 1091584 | bytes 12616 | tf_op jit(solution)/shard_map/ck,rsk->crs/dot_general | solution.py:37
  97.7 6.9 %all-to-all-done.2 = f32[32,2,1,512]{3,1,2,0:T(2,128)S(1)} async-done(((f32[32,2,1,512]{3,1,2,0:T(2,128)}), f32[32,2,1,512]{3,1,2,0:T(2,128)S(1)}, u32[]{:S(2)}, u32[]{:S(2)}) %all-to-all-start.2) | async-done | bytes 131104 | tf_op jit(solution)/shard_map/all_to_all | solution.py:63
  104.9 0.8 copy.329
  105.6 3.9 %all-to-all-start.3 = ((f32[2,32,512]{2,0,1:T(2,128)}), f32[2,32,512]{2,0,1:T(2,128)S(1)}, u32[]{:S(2)}, u32[]{:S(2)}) async-start(f32[2,32,512]{2,0,1:T(2,128)} %copy.329), calls=%async_computation.3 | async-start | bytes 262144 | tf_op jit(solution)/shard_map/all_to_all | solution.py:78
  110.1 8.5 %all-to-all-done.3 = f32[2,32,512]{2,0,1:T(2,128)S(1)} async-done(((f32[2,32,512]{2,0,1:T(2,128)}), f32[2,32,512]{2,0,1:T(2,128)S(1)}, u32[]{:S(2)}, u32[]{:S(2)}) %all-to-all-start.3) | async-done | bytes 131104 | tf_op jit(solution)/shard_map/all_to_all | solution.py:78
  118.7 7.2 %collective-permute-start.3 = (f32[2,1,7,256]{3,2,0,1:T(8,128)S(1)}, f32[2,1,7,256]{3,2,0,1:T(8,128)S(1)}, u32[]{:S(2)}, u32[]{:S(2)}) collective-permute-start(f32[2,1,7,256]{3,2,0,1:T(8,128)S(1)} %get-tuple-element.15), channel_id=1, source_target_pairs={{0,32},{32,64},{64,96},{96,128},{128,160},{160,192},{192,224},{1,3... | collective-permute-start | bytes 43016 | tf_op jit(solution)/shard_map/ppermute | solution.py:15
  125.9 2.1 %collective-permute-start.4 = (f32[2,1,7,256]{3,2,0,1:T(8,128)S(1)}, f32[2,1,7,256]{3,2,0,1:T(8,128)S(1)}, u32[]{:S(2)}, u32[]{:S(2)}) collective-permute-start(f32[2,1,7,256]{3,2,0,1:T(8,128)S(1)} %get-tuple-element.16), channel_id=1, source_target_pairs={{32,0},{64,32},{96,64},{128,96},{160,128},{192,160},{224,192},{33,... | collective-permute-start | bytes 43016 | tf_op jit(solution)/shard_map/ppermute | solution.py:18
  128.0 2.6 %fusion.13 = f32[2,128,384,1]{2,0,1,3:T(2,128)S(1)} fusion(s32[128,384]{1,0:T(8,128)S(1)} %subtract_add_fusion, f32[2,15]{1,0:T(2,128)S(1)} %rev.9), kind=kOutput, calls=%fused_computation.12 | convolution fusion | flops 19169280 | bytes 589944 | tf_op jit(solution)/shard_map/ck,rsk->crs/dot_general | solution.py:37
  131.3 0.6 fusion.25
  132.0 0.6 fusion.30
  132.9 3.4 %collective-permute-start.5 = (f32[2,1,7,256]{3,2,0,1:T(8,128)S(1)}, f32[2,1,7,256]{3,2,0,1:T(8,128)S(1)}, u32[]{:S(2)}, u32[]{:S(2)}) collective-permute-start(f32[2,1,7,256]{3,2,0,1:T(8,128)S(1)} %get-tuple-element.9), channel_id=1, source_target_pairs={{0,32},{32,64},{64,96},{96,128},{128,160},{160,192},{192,224},{1,3... | collective-permute-start | bytes 43016 | tf_op jit(solution)/shard_map/ppermute | solution.py:15
  136.3 1.9 collective-permute-start.6
  138.2 3.1 %collective-permute-done.6 = f32[2,1,7,256]{3,2,0,1:T(8,128)S(1)} collective-permute-done((f32[2,1,7,256]{3,2,0,1:T(8,128)S(1)}, f32[2,1,7,256]{3,2,0,1:T(8,128)S(1)}, u32[]{:S(2)}, u32[]{:S(2)}) %collective-permute-start.6) | collective-permute-done | bytes 14368 | tf_op jit(solution)/shard_map/ppermute | solution.py:18
  142.1 12.5 %all_to_all.56 = f32[32,2,1,512]{3,1,2,0:T(2,128)S(1)} all-to-all(f32[32,2,1,512]{3,1,2,0:T(2,128)S(1)} %constant_dynamic-update-slice_fusion.64), channel_id=1, replica_groups=mesh['tile'=8,'plane'=32] {'plane'}, dimensions={0} | all-to-all | bytes 262144 | tf_op jit(solution)/shard_map/all_to_all | solution.py:63
  155.0 12.5 %all_to_all.57 = f32[2,32,512]{2,0,1:T(2,128)S(1)} all-to-all(f32[2,32,512]{2,0,1:T(2,128)S(1)} %copy.343), channel_id=1, replica_groups=mesh['tile'=8,'plane'=32] {'plane'}, dimensions={1} | all-to-all | bytes 262144 | tf_op jit(solution)/shard_map/all_to_all | solution.py:78
  168.1 13.6 %all_to_all.58 = f32[32,2,1,512]{3,1,2,0:T(2,128)S(1)} all-to-all(f32[32,2,1,512]{3,1,2,0:T(2,128)S(1)} %constant_dynamic-update-slice_fusion.96), channel_id=1, replica_groups=mesh['tile'=8,'plane'=32] {'plane'}, dimensions={0} | all-to-all | bytes 262144 | tf_op jit(solution)/shard_map/all_to_all | solution.py:63
  182.0 12.7 %all_to_all.59 = f32[2,32,512]{2,0,1:T(2,128)S(1)} all-to-all(f32[2,32,512]{2,0,1:T(2,128)S(1)} %copy.346), channel_id=1, replica_groups=mesh['tile'=8,'plane'=32] {'plane'}, dimensions={1} | all-to-all | bytes 262144 | tf_op jit(solution)/shard_map/all_to_all | solution.py:78
  194.8 7.6 %collective-permute-start.7 = (f32[2,1,7,256]{3,2,0,1:T(8,128)S(1)}, f32[2,1,7,256]{3,2,0,1:T(8,128)S(1)}, u32[]{:S(2)}, u32[]{:S(2)}) collective-permute-start(f32[2,1,7,256]{3,2,0,1:T(8,128)S(1)} %get-tuple-element.7), channel_id=1, source_target_pairs={{0,32},{32,64},{64,96},{96,128},{128,160},{160,192},{192,224},{1,3... | collective-permute-start | bytes 43016 | tf_op jit(solution)/shard_map/ppermute | solution.py:15
  202.4 1.9 collective-permute-start.8
  204.5 2.9 %collective-permute-done.8 = f32[2,1,7,256]{3,2,0,1:T(8,128)S(1)} collective-permute-done((f32[2,1,7,256]{3,2,0,1:T(8,128)S(1)}, f32[2,1,7,256]{3,2,0,1:T(8,128)S(1)}, u32[]{:S(2)}, u32[]{:S(2)}) %collective-permute-start.8) | collective-permute-done | bytes 14368 | tf_op jit(solution)/shard_map/ppermute | solution.py:18
  207.8 0.6 fusion.35
  208.7 0.7 multiply_bitcast_fusion
  (181 shorter events, 36.5 us)
Async XLA Ops:
  0.0 9.4 %collective-permute-start = (f32[2,1,32,256]{3,2,0,1:T(8,128)}, f32[2,1,32,256]{3,2,0,1:T(8,128)S(1)}, u32[]{:S(2)}, u32[]{:S(2)}) collective-permute-start(f32[2,1,32,256]{3,2,0,1:T(8,128)} %bitcast.660), channel_id=1, source_target_pairs={{0,32},{32,64},{64,96},{96,128},{128,160},{160,192},{192,224},{1,3... | collective-permute-start | bytes 196616 | tf_op jit(solution)/shard_map/ppermute | solution.py:26
  6.0 3.4 %copy-start = (f32[2,1,64,256]{3,2,1,0:T(8,128)S(1)}, f32[2,1,64,256]{3,2,1,0:T(8,128)}, u32[]{:S(2)}) copy-start(f32[2,1,64,256]{3,2,1,0:T(8,128)} %param.6) | copy-start | bytes 393220
  10.3 4.6 %copy-start.2 = (f32[2,15]{1,0:T(2,128)S(1)}, f32[2,15]{1,0:T(2,128)}, u32[]{:S(2)}) copy-start(f32[2,15]{1,0:T(2,128)} %param.9) | copy-start | bytes 364
  10.5 4.9 %collective-permute-start.1 = (f32[2,1,7,256]{3,2,0,1:T(8,128)S(1)}, f32[2,1,7,256]{3,2,0,1:T(8,128)S(1)}, u32[]{:S(2)}, u32[]{:S(2)}) collective-permute-start(f32[2,1,7,256]{3,2,0,1:T(8,128)S(1)} %get-tuple-element.17), channel_id=1, source_target_pairs={{0,32},{32,64},{64,96},{96,128},{128,160},{160,192},{192,224},{1,3... | collective-permute-start | bytes 43016 | tf_op jit(solution)/shard_map/ppermute | solution.py:15
  12.5 5.1 %collective-permute-start.2 = (f32[2,1,7,256]{3,2,0,1:T(8,128)S(1)}, f32[2,1,7,256]{3,2,0,1:T(8,128)S(1)}, u32[]{:S(2)}, u32[]{:S(2)}) collective-permute-start(f32[2,1,7,256]{3,2,0,1:T(8,128)S(1)} %get-tuple-element.18), channel_id=1, source_target_pairs={{32,0},{64,32},{96,64},{128,96},{160,128},{192,160},{224,192},{33,... | collective-permute-start | bytes 43016 | tf_op jit(solution)/shard_map/ppermute | solution.py:18
  17.8 30.2 %copy-start.1 = (f32[2,41]{1,0:T(2,128)S(1)}, f32[2,41]{1,0:T(2,128)}, u32[]{:S(2)}) copy-start(f32[2,41]{1,0:T(2,128)} %param.8) | copy-start | bytes 988
  36.9 20.8 %all-to-all-start = ((f32[32,2,1,512]{3,1,2,0:T(2,128)}), f32[32,2,1,512]{3,1,2,0:T(2,128)S(1)}, u32[]{:S(2)}, u32[]{:S(2)}) async-start(f32[32,2,1,512]{3,1,2,0:T(2,128)} %constant_dynamic-update-slice_fusion), calls=%async_computation | async-start | bytes 262144 | tf_op jit(solution)/shard_map/all_to_all | solution.py:63
  58.8 13.0 %all-to-all-start.1 = ((f32[2,32,512]{2,0,1:T(2,128)}), f32[2,32,512]{2,0,1:T(2,128)S(1)}, u32[]{:S(2)}, u32[]{:S(2)}) async-start(f32[2,32,512]{2,0,1:T(2,128)} %copy.326), calls=%async_computation.1 | async-start | bytes 262144 | tf_op jit(solution)/shard_map/all_to_all | solution.py:78
  90.9 13.7 %all-to-all-start.2 = ((f32[32,2,1,512]{3,1,2,0:T(2,128)}), f32[32,2,1,512]{3,1,2,0:T(2,128)S(1)}, u32[]{:S(2)}, u32[]{:S(2)}) async-start(f32[32,2,1,512]{3,1,2,0:T(2,128)} %constant_dynamic-update-slice_fusion.32), calls=%async_computation.2 | async-start | bytes 262144 | tf_op jit(solution)/shard_map/all_to_all | solution.py:63
  105.6 13.0 %all-to-all-start.3 = ((f32[2,32,512]{2,0,1:T(2,128)}), f32[2,32,512]{2,0,1:T(2,128)S(1)}, u32[]{:S(2)}, u32[]{:S(2)}) async-start(f32[2,32,512]{2,0,1:T(2,128)} %copy.329), calls=%async_computation.3 | async-start | bytes 262144 | tf_op jit(solution)/shard_map/all_to_all | solution.py:78
  118.7 12.0 %collective-permute-start.3 = (f32[2,1,7,256]{3,2,0,1:T(8,128)S(1)}, f32[2,1,7,256]{3,2,0,1:T(8,128)S(1)}, u32[]{:S(2)}, u32[]{:S(2)}) collective-permute-start(f32[2,1,7,256]{3,2,0,1:T(8,128)S(1)} %get-tuple-element.15), channel_id=1, source_target_pairs={{0,32},{32,64},{64,96},{96,128},{128,160},{160,192},{192,224},{1,3... | collective-permute-start | bytes 43016 | tf_op jit(solution)/shard_map/ppermute | solution.py:15
  125.9 5.1 %collective-permute-start.4 = (f32[2,1,7,256]{3,2,0,1:T(8,128)S(1)}, f32[2,1,7,256]{3,2,0,1:T(8,128)S(1)}, u32[]{:S(2)}, u32[]{:S(2)}) collective-permute-start(f32[2,1,7,256]{3,2,0,1:T(8,128)S(1)} %get-tuple-element.16), channel_id=1, source_target_pairs={{32,0},{64,32},{96,64},{128,96},{160,128},{192,160},{224,192},{33,... | collective-permute-start | bytes 43016 | tf_op jit(solution)/shard_map/ppermute | solution.py:18
  132.9 5.4 %collective-permute-start.5 = (f32[2,1,7,256]{3,2,0,1:T(8,128)S(1)}, f32[2,1,7,256]{3,2,0,1:T(8,128)S(1)}, u32[]{:S(2)}, u32[]{:S(2)}) collective-permute-start(f32[2,1,7,256]{3,2,0,1:T(8,128)S(1)} %get-tuple-element.9), channel_id=1, source_target_pairs={{0,32},{32,64},{64,96},{96,128},{128,160},{160,192},{192,224},{1,3... | collective-permute-start | bytes 43016 | tf_op jit(solution)/shard_map/ppermute | solution.py:15
  136.3 5.1 %collective-permute-start.6 = (f32[2,1,7,256]{3,2,0,1:T(8,128)S(1)}, f32[2,1,7,256]{3,2,0,1:T(8,128)S(1)}, u32[]{:S(2)}, u32[]{:S(2)}) collective-permute-start(f32[2,1,7,256]{3,2,0,1:T(8,128)S(1)} %get-tuple-element.10), channel_id=1, source_target_pairs={{32,0},{64,32},{96,64},{128,96},{160,128},{192,160},{224,192},{33,... | collective-permute-start | bytes 43016 | tf_op jit(solution)/shard_map/ppermute | solution.py:18
  194.8 9.8 %collective-permute-start.7 = (f32[2,1,7,256]{3,2,0,1:T(8,128)S(1)}, f32[2,1,7,256]{3,2,0,1:T(8,128)S(1)}, u32[]{:S(2)}, u32[]{:S(2)}) collective-permute-start(f32[2,1,7,256]{3,2,0,1:T(8,128)S(1)} %get-tuple-element.7), channel_id=1, source_target_pairs={{0,32},{32,64},{64,96},{96,128},{128,160},{160,192},{192,224},{1,3... | collective-permute-start | bytes 43016 | tf_op jit(solution)/shard_map/ppermute | solution.py:15
  202.4 5.1 %collective-permute-start.8 = (f32[2,1,7,256]{3,2,0,1:T(8,128)S(1)}, f32[2,1,7,256]{3,2,0,1:T(8,128)S(1)}, u32[]{:S(2)}, u32[]{:S(2)}) collective-permute-start(f32[2,1,7,256]{3,2,0,1:T(8,128)S(1)} %get-tuple-element.8), channel_id=1, source_target_pairs={{32,0},{64,32},{96,64},{128,96},{160,128},{192,160},{224,192},{33,... | collective-permute-start | bytes 43016 | tf_op jit(solution)/shard_map/ppermute | solution.py:18
